TPU v7x, 32 devices: a whole 2x2x4 slice. The times are simulated.
32 devices in a mesh: ax: 8 (over z, y), rad: 4 (over x, core).
Axes of the slice: x: 2, y: 2, z: 4, core: 2. Of those that a mesh axis runs over, the one named last changes fastest.
Arguments:
- face_data: float32 [1024, 7, 5, 128], P('ax', None, None, 'rad'), may hold values from -0.6 to 0.6
- face_station: int32 [1024], P('ax'), may hold values from 0 to 511, as said below
- face_counts: int32 [8], P('ax'), may hold values from 0 to 128, as said below
- mode_slots: int32 [256], replicated, may hold values from 0 to 255, each once
- radial_proj: float32 [32, 128], P(None, 'rad'), may hold values from -0.5 to 0.5
- radial_modes: float32 [64, 32], replicated, may hold values from -1 to 1
- duct_field: float32 [32, 64, 3, 5, 2, 256], P('ax', 'rad'), may hold values from -6 to 6
- mean_mach: float32 [32, 64], P('ax', 'rad'), may hold values from 0.1 to 0.7
- pseudo_step: float32 [32, 64], P('ax', 'rad'), may hold values from 0.06 to 0.2
Outputs:
- duct_next: float32 [32, 64, 3, 5, 2, 256], P('ax', 'rad')
Inputs may be any that keep to these rules, and one draw needn't show every extreme that they name: `face_counts`: they sum to 512; one index of ax uses all 128 slots. `face_station`: slot s of ax index a is used when s < face_counts[a] and then names an angular station; each station is named by exactly one used slot; unused slots name arbitrary stations. `mode_slots`: each circumferential mode once.
All inputs are finite; a program needn't handle non-finite values.
Results may differ from a plain program's by a relative error of at most 0.00012.
Values sent between devices are 32-bit elements; how exact they have to be, the bound alone decides.
A program may use at most 128 MiB of HBM per device.

v0:
```python
import math
import jax
import jax.numpy as jnp
from jax import lax
from jax.sharding import PartitionSpec as P

NTH = 512
SAMPLE_MOMENTS = 7
HARM = 3
NMODE = 256
NRD = 64
ITERS = 3
OMEGA_STEP = 0.35
DAMPING = 0.25


def extended(cells, sides, width):
    for axis, dim in sides:
        count = lax.axis_size(axis)
        ends = count - 1
        head = lax.slice_in_dim(cells, 0, width, axis=dim)
        tail = lax.slice_in_dim(cells, cells.shape[dim] - width, cells.shape[dim], axis=dim)
        cells = jnp.concatenate(
            [
                lax.ppermute(tail, axis, [(i, (i + 1) % count) for i in range(ends)]),
                cells,
                lax.ppermute(head, axis, [((i + 1) % count, i) for i in range(ends)]),
            ],
            axis=dim,
        )
    return cells


def rotate(part):
    return jnp.stack([-part[..., 1, :], part[..., 0, :]], axis=-2)


def advance(padded, mach, step_size, inv_radius, modes):
    centre = padded[1:-1, 1:-1]
    along = (padded[2:, 1:-1] - padded[:-2, 1:-1]) * 0.5
    across = (padded[1:-1, 2:] - padded[1:-1, :-2]) * 0.5
    damped_filter = (
        padded[2:, 1:-1] + padded[:-2, 1:-1] + padded[1:-1, 2:] + padded[1:-1, :-2] - 4.0 * centre
    )
    frequency_order = jnp.arange(1, HARM + 1).astype(jnp.float32)
    omega = (OMEGA_STEP * frequency_order)[:, None, None]
    mach_cell = mach[:, :, None, None, None]
    radius_cell = inv_radius[None, :, None, None, None]
    density = centre[:, :, :, 0]
    axial = centre[:, :, :, 1]
    radial = centre[:, :, :, 2]
    swirl = centre[:, :, :, 3]
    pressure = centre[:, :, :, 4]
    source = (
        along[:, :, :, 1]
        + across[:, :, :, 2]
        + radial * radius_cell
        + rotate(swirl) * modes * radius_cell
    )
    res_density = omega * rotate(density) + mach_cell * along[:, :, :, 0] + source
    res_axial = omega * rotate(axial) + mach_cell * along[:, :, :, 1] + along[:, :, :, 4]
    res_radial = omega * rotate(radial) + mach_cell * along[:, :, :, 2] + across[:, :, :, 4]
    res_swirl = (
        omega * rotate(swirl)
        + mach_cell * along[:, :, :, 3]
        + rotate(pressure) * modes * radius_cell
    )
    res_pressure = omega * rotate(pressure) + mach_cell * along[:, :, :, 4] + source
    residual = jnp.stack([res_density, res_axial, res_radial, res_swirl, res_pressure], axis=3)
    step_cell = step_size[:, :, None, None, None, None]
    return centre - step_cell * (residual - DAMPING * damped_filter)


def project(face_data, face_station, valid, wave_orders, radial_proj):
    frequency_order = jnp.arange(1, HARM + 1)
    sample_moments = jnp.arange(SAMPLE_MOMENTS)
    revolution_count = (frequency_order[:, None] * sample_moments[None, :] % SAMPLE_MOMENTS).astype(
        jnp.float32
    ) * (2.0 * math.pi / SAMPLE_MOMENTS)
    twiddle = jnp.stack([jnp.cos(revolution_count), -jnp.sin(revolution_count)], axis=1) * (
        2.0 / SAMPLE_MOMENTS
    )
    spectral_values = jnp.einsum(
        "rtvj,kct->rkvcj", face_data, twiddle, precision=lax.Precision.HIGHEST
    )
    phase = jnp.mod(face_station[:, None] * wave_orders[None, :], NTH).astype(jnp.float32) * (
        2.0 * math.pi / NTH
    )
    cosine = jnp.where(valid[:, None], jnp.cos(phase), 0.0)
    sine = jnp.where(valid[:, None], jnp.sin(phase), 0.0)
    with_cos = jnp.einsum(
        "rs,rkvcj->kvcjs", cosine, spectral_values, precision=lax.Precision.HIGHEST
    )
    with_sin = jnp.einsum("rs,rkvcj->kvcjs", sine, spectral_values, precision=lax.Precision.HIGHEST)
    real_part = with_cos[:, :, 0] + with_sin[:, :, 1]
    imag_part = with_cos[:, :, 1] - with_sin[:, :, 0]
    fourier_transform = jnp.stack([real_part, imag_part], axis=2)
    return jnp.einsum(
        "nj,kvcjs->nkvcs", radial_proj, fourier_transform, precision=lax.Precision.HIGHEST
    )


def on_device(
    face_data,
    face_station,
    face_counts,
    mode_slots,
    radial_proj,
    radial_modes,
    duct_field,
    mean_mach,
    pseudo_step,
):
    slot_ids = jnp.arange(face_station.shape[0])
    valid = slot_ids < face_counts[0]
    wave_orders = mode_slots - NMODE // 2
    partial_value = project(face_data, face_station, valid, wave_orders, radial_proj)
    rows_here = duct_field.shape[1]
    radial_index = lax.axis_index("rad")
    totals = lax.psum(partial_value, ("ax", "rad"))
    shape_rows = lax.dynamic_slice_in_dim(radial_modes, radial_index * rows_here, rows_here, 0)
    boundary = jnp.einsum("jn,nkvcs->jkvcs", shape_rows, totals, precision=lax.Precision.HIGHEST)
    modes = wave_orders.astype(jnp.float32)
    radial_start = radial_index * rows_here
    global_rows = (radial_start + jnp.arange(rows_here)).astype(jnp.float32)
    inv_radius = 1.0 / (NRD + global_rows + 0.5)
    at_inlet = lax.axis_index("ax") == 0
    field = duct_field
    for sweep in range(ITERS):
        padded = extended(field, (("ax", 0), ("rad", 1)), 1)
        ghost = jnp.where(at_inlet, boundary, padded[0, 1:-1])
        padded = padded.at[0, 1:-1].set(ghost)
        field = advance(padded, mean_mach, pseudo_step, inv_radius, modes)
    return field


def solution(mesh):
    in_specs = (
        P("ax", None, None, "rad"),
        P("ax"),
        P("ax"),
        P(),
        P(None, "rad"),
        P(),
        P("ax", "rad", None, None, None, None),
        P("ax", "rad"),
        P("ax", "rad"),
    )
    out_specs = P("ax", "rad", None, None, None, None)
    return jax.shard_map(
        on_device, mesh=mesh, in_specs=in_specs, out_specs=out_specs, check_vma=False
    )
```

profile of v0, /device:TPU:9, one launch (start us, length us, event | category | flops | bytes accessed | tf_op | source)
XLA Modules:
  0.0 296.3 jit_solution(11995770886220923457)
XLA Ops:
  7.8 3.3 %collective-permute-start = (f32[1,16,3,5,2,256]{5,1,2,4,3,0:T(8,128)S(1)}, f32[1,16,3,5,2,256]{5,1,2,4,3,0:T(8,128)S(1)}, u32[]{:S(2)}, u32[]{:S(2)}) collective-permute-start(f32[1,16,3,5,2,256]{5,1,2,4,3,0:T(8,128)S(1)} %copy.42), channel_id=1, source_target_pairs={{0,4},{4,8},{8,12},{12,16},{16,20},{20,24},{24,28},{1,5},{5,9},{9,... | collective-permute-start | bytes 1474568 | tf_op jit(solution)/shard_map/ppermute | solution.py:25
  13.8 3.0 %collective-permute-start.1 = (f32[1,16,3,5,2,256]{5,1,2,0,4,3:T(8,128)}, f32[1,16,3,5,2,256]{5,1,2,0,4,3:T(8,128)S(1)}, u32[]{:S(2)}, u32[]{:S(2)}) collective-permute-start(f32[1,16,3,5,2,256]{5,1,2,0,4,3:T(8,128)} %slice.556), channel_id=1, source_target_pairs={{4,0},{8,4},{12,8},{16,12},{20,16},{24,20},{28,24},{5,1},{9,5},{13... | collective-permute-start | bytes 1474568 | tf_op jit(solution)/shard_map/ppermute | solution.py:27
  24.7 7.5 %collective-permute-done = f32[1,16,3,5,2,256]{5,1,2,4,3,0:T(8,128)S(1)} collective-permute-done((f32[1,16,3,5,2,256]{5,1,2,4,3,0:T(8,128)S(1)}, f32[1,16,3,5,2,256]{5,1,2,4,3,0:T(8,128)S(1)}, u32[]{:S(2)}, u32[]{:S(2)}) %collective-permute-start) | collective-permute-done | bytes 491552 | tf_op jit(solution)/shard_map/ppermute | solution.py:25
  32.2 2.9 collective-permute-done.1
  36.2 3.5 %collective-permute-start.2 = (f32[6,1,3,5,2,256]{5,1,2,0,4,3:T(1,128)}, f32[6,1,3,5,2,256]{5,1,2,0,4,3:T(1,128)}, u32[]{:S(2)}, u32[]{:S(2)}) collective-permute-start(f32[6,1,3,5,2,256]{5,1,2,0,4,3:T(1,128)} %get-tuple-element.76), channel_id=1, source_target_pairs={{0,1},{1,2},{2,3},{4,5},{5,6},{6,7},{8,9},{9,10},{10,11},{12,13},{... | collective-permute-start | bytes 552968 | tf_op jit(solution)/shard_map/ppermute | solution.py:25
  41.6 112.0 %all-reduce.2.cloned.1.call-done = f32[32,3,5,2,256]{4,0,3,2,1:T(8,128)} async-done(((f32[32,3,5,2,256]{4,0,3,2,1:T(8,128)}), f32[32,3,5,2,256]{4,0,3,2,1:T(8,128)}) %all-reduce.2.cloned.1.call-update) | async-done | bytes 983056 | tf_op jit(solution)/shard_map/psum | solution.py:120
  156.3 3.8 %pad_maximum_fusion = f32[6,18,3,5,2,256]{5,1,2,0,4,3:T(8,128)} fusion(f32[6,1,3,5,2,256]{5,1,2,0,4,3:T(1,128)} %collective-permute-done.3, f32[1,16,3,5,2,256]{5,1,2,0,4,3:T(8,128)S(1)} %collective-permute-done.1, f32[4,16,3,5,2,256]{5,1,2,0,4,3:T(8,128)S(1)} %copy.13, f32[1,16,3,5,2,256]{5,1,2,0,4,3:T(8,128)S(1)} %bitcast.166, ...), kind=kLoop, calls=%fused_computation | loop fusion | flops 3317760 | bytes 6635520 | tf_op jit(solution)/shard_map/concatenate | solution.py:23
  160.2 5.0 %scatter.10 = f32[6,18,3,5,2,256]{5,1,2,0,4,3:T(8,128)} dynamic-update-slice(f32[6,18,3,5,2,256]{5,1,2,0,4,3:T(8,128)} %pad_maximum_fusion, f32[1,16,3,5,2,256]{5,1,2,0,4,3:T(8,128)} %fusion.7, s32[]{:T(128)} %bitcast.17, s32[]{:T(128)} %bitcast.18, s32[]{:T(128)} %constant.117.clone.1, s32[]{:T(128)} %constant.117.clone.1, s32[]{:T(128)} %constant.117.clone.1, s32[]{:T(128)} %constant.117.clone.1) | dynamic-update-slice | bytes 983044 | tf_op jit(solution)/shard_map/scatter | solution.py:132
  167.5 5.5 %subtract_multiply_fusion.5 = (f32[4,16,3,5,2,256]{5,1,2,0,4,3:T(8,128)S(1)}, f32[4,16,3,5,2,256]{5,1,2,0,4,3:T(8,128)S(1)}) fusion(f32[6,18,3,5,2,256]{5,1,2,0,4,3:T(8,128)} %scatter.10), kind=kLoop, calls=%fused_computation.11 | loop fusion | flops 1966080 | bytes 11796480 | tf_op jit(solution)/shard_map/mul | solution.py:41
  176.0 3.2 %collective-permute-start.4 = (f32[1,16,3,5,2,256]{5,1,2,4,3,0:T(8,128)S(1)}, f32[1,16,3,5,2,256]{5,1,2,4,3,0:T(8,128)S(1)}, u32[]{:S(2)}, u32[]{:S(2)}) collective-permute-start(f32[1,16,3,5,2,256]{5,1,2,4,3,0:T(8,128)S(1)} %get-tuple-element.80), channel_id=1, source_target_pairs={{0,4},{4,8},{8,12},{12,16},{16,20},{20,24},{24,28},{1,5},{5,9},{9,... | collective-permute-start | bytes 1474568 | tf_op jit(solution)/shard_map/ppermute | solution.py:25
  179.2 3.1 %collective-permute-start.5 = (f32[1,16,3,5,2,256]{5,1,2,0,4,3:T(8,128)S(1)}, f32[1,16,3,5,2,256]{5,1,2,0,4,3:T(8,128)S(1)}, u32[]{:S(2)}, u32[]{:S(2)}) collective-permute-start(f32[1,16,3,5,2,256]{5,1,2,0,4,3:T(8,128)S(1)} %get-tuple-element.81), channel_id=1, source_target_pairs={{4,0},{8,4},{12,8},{16,12},{20,16},{24,20},{28,24},{5,1},{9,5},{13... | collective-permute-start | bytes 1474568 | tf_op jit(solution)/shard_map/ppermute | solution.py:27
  182.4 15.3 %collective-permute-done.4 = f32[1,16,3,5,2,256]{5,1,2,4,3,0:T(8,128)S(1)} collective-permute-done((f32[1,16,3,5,2,256]{5,1,2,4,3,0:T(8,128)S(1)}, f32[1,16,3,5,2,256]{5,1,2,4,3,0:T(8,128)S(1)}, u32[]{:S(2)}, u32[]{:S(2)}) %collective-permute-start.4) | collective-permute-done | bytes 491552 | tf_op jit(solution)/shard_map/ppermute | solution.py:25
  197.7 5.0 %collective-permute-done.5 = f32[1,16,3,5,2,256]{5,1,2,0,4,3:T(8,128)S(1)} collective-permute-done((f32[1,16,3,5,2,256]{5,1,2,0,4,3:T(8,128)S(1)}, f32[1,16,3,5,2,256]{5,1,2,0,4,3:T(8,128)S(1)}, u32[]{:S(2)}, u32[]{:S(2)}) %collective-permute-start.5) | collective-permute-done | bytes 491552 | tf_op jit(solution)/shard_map/ppermute | solution.py:27
  202.9 3.5 %collective-permute-start.6 = (f32[6,1,3,5,2,256]{5,1,2,0,4,3:T(1,128)S(1)}, f32[6,1,3,5,2,256]{5,1,2,0,4,3:T(1,128)S(1)}, u32[]{:S(2)}, u32[]{:S(2)}) collective-permute-start(f32[6,1,3,5,2,256]{5,1,2,0,4,3:T(1,128)S(1)} %get-tuple-element.74), channel_id=1, source_target_pairs={{0,1},{1,2},{2,3},{4,5},{5,6},{6,7},{8,9},{9,10},{10,11},{12,13},{... | collective-permute-start | bytes 552968 | tf_op jit(solution)/shard_map/ppermute | solution.py:25
  208.8 4.4 %collective-permute-done.7 = f32[6,1,3,5,2,256]{5,1,2,0,4,3:T(1,128)S(1)} collective-permute-done((f32[6,1,3,5,2,256]{5,1,2,0,4,3:T(1,128)S(1)}, f32[6,1,3,5,2,256]{5,1,2,0,4,3:T(1,128)S(1)}, u32[]{:S(2)}, u32[]{:S(2)}) %collective-permute-start.7) | collective-permute-done | bytes 184352 | tf_op jit(solution)/shard_map/ppermute | solution.py:27
  213.2 2.9 pad_maximum_fusion.1
  216.1 4.9 %scatter.11 = f32[6,18,3,5,2,256]{5,1,2,0,4,3:T(8,128)} dynamic-update-slice(f32[6,18,3,5,2,256]{5,1,2,0,4,3:T(8,128)} %pad_maximum_fusion.1, f32[1,16,3,5,2,256]{5,1,2,0,4,3:T(8,128)S(1)} %fusion.6, s32[]{:T(128)} %bitcast.17, s32[]{:T(128)} %bitcast.18, s32[]{:T(128)} %constant.117.clone.1, s32[]{:T(128)} %constant.117.clone.1, s32[]{:T(128)} %constant.117.clone.1, s32[]{:T(128)} %constant.117.clone.1) | dynamic-update-slice | bytes 983044 | tf_op jit(solution)/shard_map/scatter | solution.py:132
  223.2 6.6 %fusion.116 = (f32[4,16,3,5,2,256]{5,1,2,0,4,3:T(8,128)S(1)}, f32[4,16,3,5,2,256]{5,1,2,0,4,3:T(8,128)S(1)}, f32[4,16,3,5,2,256]{5,1,2,0,4,3:T(8,128)S(1)}) fusion(f32[6,18,3,5,2,256]{5,1,2,0,4,3:T(8,128)} %scatter.11), kind=kLoop, calls=%fused_computation.232 | loop fusion | flops 1966080 | bytes 15728640 | tf_op jit(solution)/shard_map/slice | solution.py:39
  234.0 4.3 %collective-permute-start.9 = (f32[1,16,3,5,2,256]{5,1,4,3,2,0:T(8,128)S(1)}, f32[1,16,3,5,2,256]{5,1,4,3,2,0:T(8,128)S(1)}, u32[]{:S(2)}, u32[]{:S(2)}) collective-permute-start(f32[1,16,3,5,2,256]{5,1,4,3,2,0:T(8,128)S(1)} %get-tuple-element.79), channel_id=1, source_target_pairs={{4,0},{8,4},{12,8},{16,12},{20,16},{24,20},{28,24},{5,1},{9,5},{13... | collective-permute-start | bytes 1474568 | tf_op jit(solution)/shard_map/ppermute | solution.py:27
  238.2 14.1 %collective-permute-done.8 = f32[1,16,3,5,2,256]{5,1,4,3,2,0:T(8,128)S(1)} collective-permute-done((f32[1,16,3,5,2,256]{5,1,4,3,2,0:T(8,128)S(1)}, f32[1,16,3,5,2,256]{5,1,4,3,2,0:T(8,128)S(1)}, u32[]{:S(2)}, u32[]{:S(2)}) %collective-permute-start.8) | collective-permute-done | bytes 491552 | tf_op jit(solution)/shard_map/ppermute | solution.py:25
  252.4 3.1 %collective-permute-done.9 = f32[1,16,3,5,2,256]{5,1,4,3,2,0:T(8,128)S(1)} collective-permute-done((f32[1,16,3,5,2,256]{5,1,4,3,2,0:T(8,128)S(1)}, f32[1,16,3,5,2,256]{5,1,4,3,2,0:T(8,128)S(1)}, u32[]{:S(2)}, u32[]{:S(2)}) %collective-permute-start.9) | collective-permute-done | bytes 491552 | tf_op jit(solution)/shard_map/ppermute | solution.py:27
  260.4 4.1 %collective-permute-done.11 = f32[6,1,3,5,2,256]{5,1,4,3,2,0:T(1,128)S(1)} collective-permute-done((f32[6,1,3,5,2,256]{5,1,4,3,2,0:T(1,128)S(1)}, f32[6,1,3,5,2,256]{5,1,4,3,2,0:T(1,128)S(1)}, u32[]{:S(2)}, u32[]{:S(2)}) %collective-permute-start.11) | collective-permute-done | bytes 184352 | tf_op jit(solution)/shard_map/ppermute | solution.py:27
  267.3 4.9 %scatter.14 = f32[6,18,3,5,2,256]{5,1,4,3,2,0:T(8,128)} dynamic-update-slice(f32[6,18,3,5,2,256]{5,1,4,3,2,0:T(8,128)} %pad_maximum_fusion.2, f32[1,16,3,5,2,256]{5,1,4,3,2,0:T(8,128)S(1)} %fusion.5, s32[]{:T(128)} %bitcast.17, s32[]{:T(128)} %bitcast.18, s32[]{:T(128)} %constant.117.clone.1, s32[]{:T(128)} %constant.117.clone.1, s32[]{:T(128)} %constant.117.clone.1, s32[]{:T(128)} %constant.117.clone.1) | dynamic-update-slice | bytes 983044 | tf_op jit(solution)/shard_map/scatter | solution.py:132
  272.2 3.1 %slice_bitcast_fusion.1 = (f32[4,16,3,2,256]{4,1,3,2,0:T(8,128)S(1)}, f32[4,16,3,1,2,256]{5,1,4,3,2,0:T(8,128)}, f32[4,16,3,1,2,256]{5,1,4,3,2,0:T(8,128)}, f32[...) fusion(f32[6,18,3,5,2,256]{5,1,4,3,2,0:T(8,128)} %scatter.14), kind=kLoop, calls=%fused_computation.29 | loop fusion | bytes 3932160 | tf_op jit(solution)/shard_map/squeeze | solution.py:53
  (115 shorter events, 52.5 us)
Async XLA Ops:
  6.5 15.5 %copy-start = (f32[32,32]{1,0:T(8,128)S(1)}, f32[32,32]{1,0:T(8,128)}, u32[]{:S(2)}) copy-start(f32[32,32]{1,0:T(8,128)} %param.19) | copy-start | bytes 12292
  6.5 147.1 %all-reduce.2.cloned.1.call-start = ((), (), s32[]{:S(2)}) async-start(), calls=%async_computation | async-start | bytes 1966080 | tf_op jit(solution)/shard_map/psum | solution.py:120
  7.8 9.7 %copy-start.12 = (s32[256]{0:T(256)S(1)}, s32[256]{0:T(256)}, u32[]{:S(2)}) copy-start(s32[256]{0:T(256)} %param.18) | copy-start | bytes 3076
  7.8 9.8 %copy-start.7 = (f32[128,7,5,32]{0,3,2,1:T(8,128)S(1)}, f32[128,7,5,32]{0,3,2,1:T(8,128)}, u32[]{:S(2)}) copy-start(f32[128,7,5,32]{0,3,2,1:T(8,128)} %param.15) | copy-start | bytes 1720324
  7.8 24.4 %collective-permute-start = (f32[1,16,3,5,2,256]{5,1,2,4,3,0:T(8,128)S(1)}, f32[1,16,3,5,2,256]{5,1,2,4,3,0:T(8,128)S(1)}, u32[]{:S(2)}, u32[]{:S(2)}) collective-permute-start(f32[1,16,3,5,2,256]{5,1,2,4,3,0:T(8,128)S(1)} %copy.42), channel_id=1, source_target_pairs={{0,4},{4,8},{8,12},{12,16},{16,20},{20,24},{24,28},{1,5},{5,9},{9,... | collective-permute-start | bytes 1474568 | tf_op jit(solution)/shard_map/ppermute | solution.py:25
  13.0 5.9 %copy-start.11 = (s32[128]{0:T(128)S(1)}, s32[128]{0:T(128)}, u32[]{:S(2)}) copy-start(s32[128]{0:T(128)} %param.16) | copy-start | bytes 1540
  13.8 21.3 %collective-permute-start.1 = (f32[1,16,3,5,2,256]{5,1,2,0,4,3:T(8,128)}, f32[1,16,3,5,2,256]{5,1,2,0,4,3:T(8,128)S(1)}, u32[]{:S(2)}, u32[]{:S(2)}) collective-permute-start(f32[1,16,3,5,2,256]{5,1,2,0,4,3:T(8,128)} %slice.556), channel_id=1, source_target_pairs={{4,0},{8,4},{12,8},{16,12},{20,16},{24,20},{28,24},{5,1},{9,5},{13... | collective-permute-start | bytes 1474568 | tf_op jit(solution)/shard_map/ppermute | solution.py:27
  24.0 129.7 %copy-start.10 = (f32[64,32]{0,1:T(8,128)S(1)}, f32[64,32]{0,1:T(8,128)}, u32[]{:S(2)}) copy-start(f32[64,32]{0,1:T(8,128)} %param.20) | copy-start | bytes 24580
  36.2 120.2 %collective-permute-start.2 = (f32[6,1,3,5,2,256]{5,1,2,0,4,3:T(1,128)}, f32[6,1,3,5,2,256]{5,1,2,0,4,3:T(1,128)}, u32[]{:S(2)}, u32[]{:S(2)}) collective-permute-start(f32[6,1,3,5,2,256]{5,1,2,0,4,3:T(1,128)} %get-tuple-element.76), channel_id=1, source_target_pairs={{0,1},{1,2},{2,3},{4,5},{5,6},{6,7},{8,9},{9,10},{10,11},{12,13},{... | collective-permute-start | bytes 552968 | tf_op jit(solution)/shard_map/ppermute | solution.py:25
  39.7 116.7 %collective-permute-start.3 = (f32[6,1,3,5,2,256]{5,1,2,0,4,3:T(1,128)}, f32[6,1,3,5,2,256]{5,1,2,0,4,3:T(1,128)}, u32[]{:S(2)}, u32[]{:S(2)}) collective-permute-start(f32[6,1,3,5,2,256]{5,1,2,0,4,3:T(1,128)} %get-tuple-element.77), channel_id=1, source_target_pairs={{1,0},{2,1},{3,2},{5,4},{6,5},{7,6},{9,8},{10,9},{11,10},{13,12},{... | collective-permute-start | bytes 552968 | tf_op jit(solution)/shard_map/ppermute | solution.py:27
  165.2 8.0 %slice-start.2 = ((s8[4423680]{0:T(1024)(128)(4,1)}), s8[4194304]{0:T(1024)(128)(4,1)S(1)}, s32[]{:S(2)}) async-start(s8[4423680]{0:T(1024)(128)(4,1)} %bitcast.163), calls=%async_computation.3 | async-start | bytes 8388608
  167.5 5.7 %slice-start.3 = ((s8[4423680]{0:T(1024)(128)(4,1)}), s8[229376]{0:T(1024)(128)(4,1)S(1)}, s32[]{:S(2)}) async-start(s8[4423680]{0:T(1024)(128)(4,1)} %bitcast.163), calls=%async_computation.4 | async-start | bytes 458752
  176.0 21.7 %collective-permute-start.4 = (f32[1,16,3,5,2,256]{5,1,2,4,3,0:T(8,128)S(1)}, f32[1,16,3,5,2,256]{5,1,2,4,3,0:T(8,128)S(1)}, u32[]{:S(2)}, u32[]{:S(2)}) collective-permute-start(f32[1,16,3,5,2,256]{5,1,2,4,3,0:T(8,128)S(1)} %get-tuple-element.80), channel_id=1, source_target_pairs={{0,4},{4,8},{8,12},{12,16},{16,20},{20,24},{24,28},{1,5},{5,9},{9,... | collective-permute-start | bytes 1474568 | tf_op jit(solution)/shard_map/ppermute | solution.py:25
  179.2 23.4 %collective-permute-start.5 = (f32[1,16,3,5,2,256]{5,1,2,0,4,3:T(8,128)S(1)}, f32[1,16,3,5,2,256]{5,1,2,0,4,3:T(8,128)S(1)}, u32[]{:S(2)}, u32[]{:S(2)}) collective-permute-start(f32[1,16,3,5,2,256]{5,1,2,0,4,3:T(8,128)S(1)} %get-tuple-element.81), channel_id=1, source_target_pairs={{4,0},{8,4},{12,8},{16,12},{20,16},{24,20},{28,24},{5,1},{9,5},{13... | collective-permute-start | bytes 1474568 | tf_op jit(solution)/shard_map/ppermute | solution.py:27
  202.9 5.9 %collective-permute-start.6 = (f32[6,1,3,5,2,256]{5,1,2,0,4,3:T(1,128)S(1)}, f32[6,1,3,5,2,256]{5,1,2,0,4,3:T(1,128)S(1)}, u32[]{:S(2)}, u32[]{:S(2)}) collective-permute-start(f32[6,1,3,5,2,256]{5,1,2,0,4,3:T(1,128)S(1)} %get-tuple-element.74), channel_id=1, source_target_pairs={{0,1},{1,2},{2,3},{4,5},{5,6},{6,7},{8,9},{9,10},{10,11},{12,13},{... | collective-permute-start | bytes 552968 | tf_op jit(solution)/shard_map/ppermute | solution.py:25
  206.4 6.9 %collective-permute-start.7 = (f32[6,1,3,5,2,256]{5,1,2,0,4,3:T(1,128)S(1)}, f32[6,1,3,5,2,256]{5,1,2,0,4,3:T(1,128)S(1)}, u32[]{:S(2)}, u32[]{:S(2)}) collective-permute-start(f32[6,1,3,5,2,256]{5,1,2,0,4,3:T(1,128)S(1)} %get-tuple-element.75), channel_id=1, source_target_pairs={{1,0},{2,1},{3,2},{5,4},{6,5},{7,6},{9,8},{10,9},{11,10},{13,12},{... | collective-permute-start | bytes 552968 | tf_op jit(solution)/shard_map/ppermute | solution.py:27
  221.0 9.0 %slice-start = ((s8[4423680]{0:T(1024)(128)(4,1)}), s8[4194304]{0:T(1024)(128)(4,1)S(1)}, s32[]{:S(2)}) async-start(s8[4423680]{0:T(1024)(128)(4,1)} %bitcast.161), calls=%async_computation.1 | async-start | bytes 8388608
  223.2 6.8 %slice-start.1 = ((s8[4423680]{0:T(1024)(128)(4,1)}), s8[229376]{0:T(1024)(128)(4,1)S(1)}, s32[]{:S(2)}) async-start(s8[4423680]{0:T(1024)(128)(4,1)} %bitcast.161), calls=%async_computation.2 | async-start | bytes 458752
  232.0 20.3 %collective-permute-start.8 = (f32[1,16,3,5,2,256]{5,1,4,3,2,0:T(8,128)S(1)}, f32[1,16,3,5,2,256]{5,1,4,3,2,0:T(8,128)S(1)}, u32[]{:S(2)}, u32[]{:S(2)}) collective-permute-start(f32[1,16,3,5,2,256]{5,1,4,3,2,0:T(8,128)S(1)} %get-tuple-element.78), channel_id=1, source_target_pairs={{0,4},{4,8},{8,12},{12,16},{16,20},{20,24},{24,28},{1,5},{5,9},{9,... | collective-permute-start | bytes 1474568 | tf_op jit(solution)/shard_map/ppermute | solution.py:25
  234.0 21.5 %collective-permute-start.9 = (f32[1,16,3,5,2,256]{5,1,4,3,2,0:T(8,128)S(1)}, f32[1,16,3,5,2,256]{5,1,4,3,2,0:T(8,128)S(1)}, u32[]{:S(2)}, u32[]{:S(2)}) collective-permute-start(f32[1,16,3,5,2,256]{5,1,4,3,2,0:T(8,128)S(1)} %get-tuple-element.79), channel_id=1, source_target_pairs={{4,0},{8,4},{12,8},{16,12},{20,16},{24,20},{28,24},{5,1},{9,5},{13... | collective-permute-start | bytes 1474568 | tf_op jit(solution)/shard_map/ppermute | solution.py:27
  255.7 4.7 %collective-permute-start.10 = (f32[6,1,3,5,2,256]{5,1,4,3,2,0:T(1,128)S(1)}, f32[6,1,3,5,2,256]{5,1,4,3,2,0:T(1,128)S(1)}, u32[]{:S(2)}, u32[]{:S(2)}) collective-permute-start(f32[6,1,3,5,2,256]{5,1,4,3,2,0:T(1,128)S(1)} %get-tuple-element.72), channel_id=1, source_target_pairs={{0,1},{1,2},{2,3},{4,5},{5,6},{6,7},{8,9},{9,10},{10,11},{12,13},{... | collective-permute-start | bytes 552968 | tf_op jit(solution)/shard_map/ppermute | solution.py:25
  257.6 6.9 %collective-permute-start.11 = (f32[6,1,3,5,2,256]{5,1,4,3,2,0:T(1,128)S(1)}, f32[6,1,3,5,2,256]{5,1,4,3,2,0:T(1,128)S(1)}, u32[]{:S(2)}, u32[]{:S(2)}) collective-permute-start(f32[6,1,3,5,2,256]{5,1,4,3,2,0:T(1,128)S(1)} %get-tuple-element.73), channel_id=1, source_target_pairs={{1,0},{2,1},{3,2},{5,4},{6,5},{7,6},{9,8},{10,9},{11,10},{13,12},{... | collective-permute-start | bytes 552968 | tf_op jit(solution)/shard_map/ppermute | solution.py:27
  272.2 3.2 %copy-start.2 = (f32[6,18,3,5,2,256]{5,1,4,3,2,0:T(8,128)S(1)}, f32[6,18,3,5,2,256]{5,1,4,3,2,0:T(8,128)}, u32[]{:S(2)}) copy-start(f32[6,18,3,5,2,256]{5,1,4,3,2,0:T(8,128)} %scatter.14) | copy-start | bytes 9953284
  285.1 4.3 %copy-start.1 = (f32[32,32]{1,0:T(8,128)S(1)}, f32[32,32]{1,0:T(8,128)}, u32[]{:S(2)}) copy-start(f32[32,32]{1,0:T(8,128)} %param.19) | copy-start | bytes 12292
  (6 other events, 7.6 us)
Sparse Core Ops, SparseCore 0:
  24.1 129.4 all-reduce.1
where the time goes:
time: 297 us; the launch traced here: 296 us
  waiting for transfers between devices  169 us (57%)
  local copies, waits for them, and re-layouts  38.5 us (13%)
  starting transfers between devices  34.2 us (12%)
  other arithmetic  32.1 us (11%)
  between operations  14.7 us (5%)
  matrix products  7.93 us (3%)
    psum x1, waiting for transfers between devices, on_device(): totals = lax.psum(partial_value, ('ax', 'rad'))  112 us
    ppermute x6, waiting for transfers between devices, extended(): lax.ppermute(tail, axis, [(i, (i + 1) % count) for i in range(ends)])  37.4 us
    ppermute x6, waiting for transfers between devices, extended(): lax.ppermute(head, axis, [((i + 1) % count, i) for i in range(ends)])  19.5 us
    ppermute x6, starting transfers between devices, extended(): lax.ppermute(tail, axis, [(i, (i + 1) % count) for i in range(ends)])  17.3 us
    ppermute x6, starting transfers between devices, extended(): lax.ppermute(head, axis, [((i + 1) % count, i) for i in range(ends)])  16.9 us
    scatter x3, local copies, waits for them, and re-layouts, on_device(): padded = padded.at[0, 1:-1].set(ghost)  14.8 us
    concatenate x3, other arithmetic, extended(): jnp.concatenate([lax.ppermute(tail, axis, [(i, (i + 1) % count) for i in...  9.55 us
    unnamed x40, local copies, waits for them, and re-layouts  7.62 us
  transfers between devices with their start and end apart: 13, of which 10 were waited for; matrix products, arithmetic and copies ran while one was open for 5% of the time, Pallas kernels for 0%

commit v1 on v0

--- a/solution.py
+++ b/solution.py
@@ -117,7 +117,9 @@
     partial_value = project(face_data, face_station, valid, wave_orders, radial_proj)
     rows_here = duct_field.shape[1]
     radial_index = lax.axis_index("rad")
-    totals = lax.psum(partial_value, ("ax", "rad"))
+    totals = partial_value
+    for mesh_axis in ("rad", "ax"):
+        totals = lax.psum(totals, mesh_axis)
     shape_rows = lax.dynamic_slice_in_dim(radial_modes, radial_index * rows_here, rows_here, 0)
     boundary = jnp.einsum("jn,nkvcs->jkvcs", shape_rows, totals, precision=lax.Precision.HIGHEST)
     modes = wave_orders.astype(jnp.float32)

time: 297 us -> 271 us (0.912)
  waiting for transfers between devices: 169 us -> 145 us
    psum x1 -> x2, waiting for transfers between devices: 112 us -> 93.7 us  [on_device(): totals = lax.psum(totals, mesh_axis)]
    ppermute x6, waiting for transfers between devices: 37.4 us -> 31.7 us  [extended(): lax.ppermute(tail, axis, [(i, (i + 1) % count) for i in range(ends)])]
    unnamed x40 -> x36, local copies, waits for them, and re-layouts: 7.62 us -> 8.42 us
  transfers between devices with their start and end apart: 13 -> 14, of which waited for: 10 -> 10; matrix products, arithmetic and copies ran while one was open for 5% -> 2% of each run, Pallas kernels for 0% -> 0%
where the time goes in v1:
time: 271 us; the launch traced here: 270 us
  waiting for transfers between devices  145 us (54%)
  local copies, waits for them, and re-layouts  37 us (14%)
  starting transfers between devices  33.9 us (13%)
  other arithmetic  30.2 us (11%)
  between operations  14.7 us (5%)
  matrix products  9.64 us (4%)
    psum x2, waiting for transfers between devices, on_device(): totals = lax.psum(totals, mesh_axis)  93.7 us
    ppermute x6, waiting for transfers between devices, extended(): lax.ppermute(tail, axis, [(i, (i + 1) % count) for i in range(ends)])  31.7 us
    ppermute x6, waiting for transfers between devices, extended(): lax.ppermute(head, axis, [((i + 1) % count, i) for i in range(ends)])  19.3 us
    ppermute x6, starting transfers between devices, extended(): lax.ppermute(tail, axis, [(i, (i + 1) % count) for i in range(ends)])  17.7 us
    ppermute x6, starting transfers between devices, extended(): lax.ppermute(head, axis, [((i + 1) % count, i) for i in range(ends)])  16.1 us
    scatter x3, local copies, waits for them, and re-layouts, on_device(): padded = padded.at[0, 1:-1].set(ghost)  14.7 us
    concatenate x3, other arithmetic, extended(): jnp.concatenate([lax.ppermute(tail, axis, [(i, (i + 1) % count) for i in...  8.6 us
    unnamed x36, local copies, waits for them, and re-layouts  8.42 us
  transfers between devices with their start and end apart: 14, of which 10 were waited for; matrix products, arithmetic and copies ran while one was open for 2% of the time, Pallas kernels for 0%

profile of v1, /device:TPU:9, one launch (start us, length us, event | category | flops | bytes accessed | tf_op | source)
XLA Modules:
  0.0 270.3 jit_solution(2436010545151979610)
XLA Ops:
  17.0 3.1 %collective-permute-start = (f32[1,16,3,5,2,256]{5,1,2,4,3,0:T(8,128)}, f32[1,16,3,5,2,256]{5,1,2,4,3,0:T(8,128)S(1)}, u32[]{:S(2)}, u32[]{:S(2)}) collective-permute-start(f32[1,16,3,5,2,256]{5,1,2,4,3,0:T(8,128)} %copy.42), channel_id=1, source_target_pairs={{0,4},{4,8},{8,12},{12,16},{16,20},{20,24},{24,28},{1,5},{5,9},{9,... | collective-permute-start | bytes 1474568 | tf_op jit(solution)/shard_map/ppermute | solution.py:25
  22.0 3.0 %collective-permute-start.1 = (f32[1,16,3,5,2,256]{5,1,2,0,4,3:T(8,128)S(1)}, f32[1,16,3,5,2,256]{5,1,2,0,4,3:T(8,128)S(1)}, u32[]{:S(2)}, u32[]{:S(2)}) collective-permute-start(f32[1,16,3,5,2,256]{5,1,2,0,4,3:T(8,128)S(1)} %slice.556), channel_id=1, source_target_pairs={{4,0},{8,4},{12,8},{16,12},{20,16},{24,20},{28,24},{5,1},{9,5},{13... | collective-permute-start | bytes 1474568 | tf_op jit(solution)/shard_map/ppermute | solution.py:27
  25.1 27.6 %all-reduce.3.cloned.1.call-done = f32[32,3,5,2,256]{4,0,3,2,1:T(8,128)} async-done(((f32[32,3,5,2,256]{4,0,3,2,1:T(8,128)}), f32[32,3,5,2,256]{4,0,3,2,1:T(8,128)}) %all-reduce.3.cloned.1.call-update) | async-done | bytes 983056 | tf_op jit(solution)/shard_map/psum | solution.py:122
  53.0 3.7 %collective-permute-start.2 = (f32[6,1,3,5,2,256]{5,1,2,0,4,3:T(1,128)S(1)}, f32[6,1,3,5,2,256]{5,1,2,0,4,3:T(1,128)S(1)}, u32[]{:S(2)}, u32[]{:S(2)}) collective-permute-start(f32[6,1,3,5,2,256]{5,1,2,0,4,3:T(1,128)S(1)} %get-tuple-element.76), channel_id=1, source_target_pairs={{0,1},{1,2},{2,3},{4,5},{5,6},{6,7},{8,9},{9,10},{10,11},{12,13},{... | collective-permute-start | bytes 552968 | tf_op jit(solution)/shard_map/ppermute | solution.py:25
  59.2 4.3 %collective-permute-done.3 = f32[6,1,3,5,2,256]{5,1,2,0,4,3:T(1,128)S(1)} collective-permute-done((f32[6,1,3,5,2,256]{5,1,2,0,4,3:T(1,128)S(1)}, f32[6,1,3,5,2,256]{5,1,2,0,4,3:T(1,128)S(1)}, u32[]{:S(2)}, u32[]{:S(2)}) %collective-permute-start.3) | collective-permute-done | bytes 184352 | tf_op jit(solution)/shard_map/ppermute | solution.py:27
  63.5 2.8 %pad_maximum_fusion = f32[6,18,3,5,2,256]{5,1,2,0,4,3:T(8,128)} fusion(f32[6,1,3,5,2,256]{5,1,2,0,4,3:T(1,128)S(1)} %collective-permute-done.3, f32[1,16,3,5,2,256]{5,1,2,0,4,3:T(8,128)S(1)} %collective-permute-done.1, f32[4,16,3,5,2,256]{5,1,2,0,4,3:T(8,128)S(1)} %copy.13, f32[1,16,3,5,2,256]{5,1,2,0,4,3:T(8,128)S(1)} %bitcast.166, ...), kind=kLoop, calls=%fused_computation | loop fusion | flops 3317760 | bytes 6635520 | tf_op jit(solution)/shard_map/concatenate | solution.py:23
  66.4 66.1 %all-reduce.5.cloned.1.call-done = f32[32,3,5,2,256]{4,0,3,2,1:T(8,128)} async-done(((f32[32,3,5,2,256]{4,0,3,2,1:T(8,128)}), f32[32,3,5,2,256]{4,0,3,2,1:T(8,128)}) %all-reduce.5.cloned.1.call-update) | async-done | bytes 983056 | tf_op jit(solution)/shard_map/psum | solution.py:122
  134.4 4.9 %scatter.10 = f32[6,18,3,5,2,256]{5,1,2,0,4,3:T(8,128)} dynamic-update-slice(f32[6,18,3,5,2,256]{5,1,2,0,4,3:T(8,128)} %pad_maximum_fusion, f32[1,16,3,5,2,256]{5,1,2,0,4,3:T(8,128)S(1)} %fusion.7, s32[]{:T(128)} %bitcast.17, s32[]{:T(128)} %bitcast.18, s32[]{:T(128)} %constant.117.clone.1, s32[]{:T(128)} %constant.117.clone.1, s32[]{:T(128)} %constant.117.clone.1, s32[]{:T(128)} %constant.117.clone.1) | dynamic-update-slice | bytes 983044 | tf_op jit(solution)/shard_map/scatter | solution.py:134
  141.6 5.5 %subtract_multiply_fusion.5 = (f32[4,16,3,5,2,256]{5,1,2,0,4,3:T(8,128)S(1)}, f32[4,16,3,5,2,256]{5,1,2,0,4,3:T(8,128)S(1)}) fusion(f32[6,18,3,5,2,256]{5,1,2,0,4,3:T(8,128)} %scatter.10), kind=kLoop, calls=%fused_computation.11 | loop fusion | flops 1966080 | bytes 11796480 | tf_op jit(solution)/shard_map/mul | solution.py:41
  150.1 3.2 %collective-permute-start.4 = (f32[1,16,3,5,2,256]{5,1,2,4,3,0:T(8,128)S(1)}, f32[1,16,3,5,2,256]{5,1,2,4,3,0:T(8,128)S(1)}, u32[]{:S(2)}, u32[]{:S(2)}) collective-permute-start(f32[1,16,3,5,2,256]{5,1,2,4,3,0:T(8,128)S(1)} %get-tuple-element.80), channel_id=1, source_target_pairs={{0,4},{4,8},{8,12},{12,16},{16,20},{20,24},{24,28},{1,5},{5,9},{9,... | collective-permute-start | bytes 1474568 | tf_op jit(solution)/shard_map/ppermute | solution.py:25
  153.3 3.0 %collective-permute-start.5 = (f32[1,16,3,5,2,256]{5,1,2,0,4,3:T(8,128)S(1)}, f32[1,16,3,5,2,256]{5,1,2,0,4,3:T(8,128)S(1)}, u32[]{:S(2)}, u32[]{:S(2)}) collective-permute-start(f32[1,16,3,5,2,256]{5,1,2,0,4,3:T(8,128)S(1)} %get-tuple-element.81), channel_id=1, source_target_pairs={{4,0},{8,4},{12,8},{16,12},{20,16},{24,20},{28,24},{5,1},{9,5},{13... | collective-permute-start | bytes 1474568 | tf_op jit(solution)/shard_map/ppermute | solution.py:27
  156.3 16.7 %collective-permute-done.4 = f32[1,16,3,5,2,256]{5,1,2,4,3,0:T(8,128)S(1)} collective-permute-done((f32[1,16,3,5,2,256]{5,1,2,4,3,0:T(8,128)S(1)}, f32[1,16,3,5,2,256]{5,1,2,4,3,0:T(8,128)S(1)}, u32[]{:S(2)}, u32[]{:S(2)}) %collective-permute-start.4) | collective-permute-done | bytes 491552 | tf_op jit(solution)/shard_map/ppermute | solution.py:25
  173.0 3.6 %collective-permute-done.5 = f32[1,16,3,5,2,256]{5,1,2,0,4,3:T(8,128)S(1)} collective-permute-done((f32[1,16,3,5,2,256]{5,1,2,0,4,3:T(8,128)S(1)}, f32[1,16,3,5,2,256]{5,1,2,0,4,3:T(8,128)S(1)}, u32[]{:S(2)}, u32[]{:S(2)}) %collective-permute-start.5) | collective-permute-done | bytes 491552 | tf_op jit(solution)/shard_map/ppermute | solution.py:27
  176.8 3.5 %collective-permute-start.6 = (f32[6,1,3,5,2,256]{5,1,2,0,4,3:T(1,128)S(1)}, f32[6,1,3,5,2,256]{5,1,2,0,4,3:T(1,128)S(1)}, u32[]{:S(2)}, u32[]{:S(2)}) collective-permute-start(f32[6,1,3,5,2,256]{5,1,2,0,4,3:T(1,128)S(1)} %get-tuple-element.74), channel_id=1, source_target_pairs={{0,1},{1,2},{2,3},{4,5},{5,6},{6,7},{8,9},{9,10},{10,11},{12,13},{... | collective-permute-start | bytes 552968 | tf_op jit(solution)/shard_map/ppermute | solution.py:25
  182.8 4.4 %collective-permute-done.7 = f32[6,1,3,5,2,256]{5,1,2,0,4,3:T(1,128)S(1)} collective-permute-done((f32[6,1,3,5,2,256]{5,1,2,0,4,3:T(1,128)S(1)}, f32[6,1,3,5,2,256]{5,1,2,0,4,3:T(1,128)S(1)}, u32[]{:S(2)}, u32[]{:S(2)}) %collective-permute-start.7) | collective-permute-done | bytes 184352 | tf_op jit(solution)/shard_map/ppermute | solution.py:27
  190.0 4.9 %scatter.11 = f32[6,18,3,5,2,256]{5,1,2,0,4,3:T(8,128)} dynamic-update-slice(f32[6,18,3,5,2,256]{5,1,2,0,4,3:T(8,128)} %pad_maximum_fusion.1, f32[1,16,3,5,2,256]{5,1,2,0,4,3:T(8,128)S(1)} %fusion.6, s32[]{:T(128)} %bitcast.17, s32[]{:T(128)} %bitcast.18, s32[]{:T(128)} %constant.117.clone.1, s32[]{:T(128)} %constant.117.clone.1, s32[]{:T(128)} %constant.117.clone.1, s32[]{:T(128)} %constant.117.clone.1) | dynamic-update-slice | bytes 983044 | tf_op jit(solution)/shard_map/scatter | solution.py:134
  197.1 6.6 %fusion.116 = (f32[4,16,3,5,2,256]{5,1,2,0,4,3:T(8,128)S(1)}, f32[4,16,3,5,2,256]{5,1,2,0,4,3:T(8,128)S(1)}, f32[4,16,3,5,2,256]{5,1,2,0,4,3:T(8,128)S(1)}) fusion(f32[6,18,3,5,2,256]{5,1,2,0,4,3:T(8,128)} %scatter.11), kind=kLoop, calls=%fused_computation.232 | loop fusion | flops 1966080 | bytes 15728640 | tf_op jit(solution)/shard_map/slice | solution.py:39
  208.3 3.9 %collective-permute-start.9 = (f32[1,16,3,5,2,256]{5,1,4,3,2,0:T(8,128)S(1)}, f32[1,16,3,5,2,256]{5,1,4,3,2,0:T(8,128)S(1)}, u32[]{:S(2)}, u32[]{:S(2)}) collective-permute-start(f32[1,16,3,5,2,256]{5,1,4,3,2,0:T(8,128)S(1)} %get-tuple-element.79), channel_id=1, source_target_pairs={{4,0},{8,4},{12,8},{16,12},{20,16},{24,20},{28,24},{5,1},{9,5},{13... | collective-permute-start | bytes 1474568 | tf_op jit(solution)/shard_map/ppermute | solution.py:27
  212.1 14.6 %collective-permute-done.8 = f32[1,16,3,5,2,256]{5,1,4,3,2,0:T(8,128)S(1)} collective-permute-done((f32[1,16,3,5,2,256]{5,1,4,3,2,0:T(8,128)S(1)}, f32[1,16,3,5,2,256]{5,1,4,3,2,0:T(8,128)S(1)}, u32[]{:S(2)}, u32[]{:S(2)}) %collective-permute-start.8) | collective-permute-done | bytes 491552 | tf_op jit(solution)/shard_map/ppermute | solution.py:25
  234.1 4.3 %collective-permute-done.11 = f32[6,1,3,5,2,256]{5,1,4,3,2,0:T(1,128)S(1)} collective-permute-done((f32[6,1,3,5,2,256]{5,1,4,3,2,0:T(1,128)S(1)}, f32[6,1,3,5,2,256]{5,1,4,3,2,0:T(1,128)S(1)}, u32[]{:S(2)}, u32[]{:S(2)}) %collective-permute-start.11) | collective-permute-done | bytes 184352 | tf_op jit(solution)/shard_map/ppermute | solution.py:27
  238.4 2.9 %pad_maximum_fusion.2 = f32[6,18,3,5,2,256]{5,1,4,3,2,0:T(8,128)} fusion(f32[6,1,3,5,2,256]{5,1,4,3,2,0:T(1,128)S(1)} %collective-permute-done.11, f32[1,16,3,5,2,256]{5,1,4,3,2,0:T(8,128)S(1)} %collective-permute-done.9, f32[4,16,3,5,2,256]{5,1,4,3,2,0:T(8,128)S(1)} %copy_subtract_fusion, f32[1,16,3,5,2,256]{5,1,4,3,2,0:T(8,128)S(1)} %collective-permute-done.8, ...), kind=kLoop, calls=%fused_computation.2 | loop fusion | flops 3317760 | bytes 6635520 | tf_op jit(solution)/shard_map/concatenate | solution.py:23
  241.3 4.9 %scatter.14 = f32[6,18,3,5,2,256]{5,1,4,3,2,0:T(8,128)} dynamic-update-slice(f32[6,18,3,5,2,256]{5,1,4,3,2,0:T(8,128)} %pad_maximum_fusion.2, f32[1,16,3,5,2,256]{5,1,4,3,2,0:T(8,128)S(1)} %fusion.5, s32[]{:T(128)} %bitcast.17, s32[]{:T(128)} %bitcast.18, s32[]{:T(128)} %constant.117.clone.1, s32[]{:T(128)} %constant.117.clone.1, s32[]{:T(128)} %constant.117.clone.1, s32[]{:T(128)} %constant.117.clone.1) | dynamic-update-slice | bytes 983044 | tf_op jit(solution)/shard_map/scatter | solution.py:134
  246.2 3.1 %slice_bitcast_fusion.1 = (f32[4,16,3,2,256]{4,1,3,2,0:T(8,128)S(1)}, f32[4,16,3,1,2,256]{5,1,4,3,2,0:T(8,128)}, f32[4,16,3,1,2,256]{5,1,4,3,2,0:T(8,128)}, f32[...) fusion(f32[6,18,3,5,2,256]{5,1,4,3,2,0:T(8,128)} %scatter.14), kind=kLoop, calls=%fused_computation.29 | loop fusion | bytes 3932160 | tf_op jit(solution)/shard_map/squeeze | solution.py:53
  249.4 2.9 %fusion.115 = (f32[4,16,3,5,2,256]{5,1,4,3,2,0:T(8,128)}, f32[4,16,3,5,2,256]{5,1,4,3,2,0:T(8,128)S(1)}, f32[4,16,3,5,2,256]{5,1,4,3,2,0:T(8,128)S(1)}, f32[4,16...) fusion(f32[6,18,3,5,2,256]{5,1,4,3,2,0:T(8,128)S(1)} %copy-done.2), kind=kLoop, calls=%fused_computation.231 | loop fusion | bytes 19660800 | tf_op jit(solution)/shard_map/slice | solution.py:39
  (115 shorter events, 52.0 us)
Async XLA Ops:
  6.5 7.6 %copy-start = (f32[32,32]{1,0:T(8,128)S(1)}, f32[32,32]{1,0:T(8,128)}, u32[]{:S(2)}) copy-start(f32[32,32]{1,0:T(8,128)} %param.19) | copy-start | bytes 12292
  6.5 5.9 %copy-start.10 = (s32[128]{0:T(128)S(1)}, s32[128]{0:T(128)}, u32[]{:S(2)}) copy-start(s32[128]{0:T(128)} %param.16) | copy-start | bytes 1540
  6.5 46.1 %all-reduce.3.cloned.1.call-start = ((), (), s32[]{:S(2)}) async-start(), calls=%async_computation | async-start | bytes 1966080 | tf_op jit(solution)/shard_map/psum | solution.py:122
  16.1 116.4 %all-reduce.5.cloned.1.call-start = ((), (), s32[]{:S(2)}) async-start(), calls=%async_computation.1 | async-start | bytes 1966080 | tf_op jit(solution)/shard_map/psum | solution.py:122
  17.0 35.7 %collective-permute-start = (f32[1,16,3,5,2,256]{5,1,2,4,3,0:T(8,128)}, f32[1,16,3,5,2,256]{5,1,2,4,3,0:T(8,128)S(1)}, u32[]{:S(2)}, u32[]{:S(2)}) collective-permute-start(f32[1,16,3,5,2,256]{5,1,2,4,3,0:T(8,128)} %copy.42), channel_id=1, source_target_pairs={{0,4},{4,8},{8,12},{12,16},{16,20},{20,24},{24,28},{1,5},{5,9},{9,... | collective-permute-start | bytes 1474568 | tf_op jit(solution)/shard_map/ppermute | solution.py:25
  22.0 30.7 %collective-permute-start.1 = (f32[1,16,3,5,2,256]{5,1,2,0,4,3:T(8,128)S(1)}, f32[1,16,3,5,2,256]{5,1,2,0,4,3:T(8,128)S(1)}, u32[]{:S(2)}, u32[]{:S(2)}) collective-permute-start(f32[1,16,3,5,2,256]{5,1,2,0,4,3:T(8,128)S(1)} %slice.556), channel_id=1, source_target_pairs={{4,0},{8,4},{12,8},{16,12},{20,16},{24,20},{28,24},{5,1},{9,5},{13... | collective-permute-start | bytes 1474568 | tf_op jit(solution)/shard_map/ppermute | solution.py:27
  53.0 6.2 %collective-permute-start.2 = (f32[6,1,3,5,2,256]{5,1,2,0,4,3:T(1,128)S(1)}, f32[6,1,3,5,2,256]{5,1,2,0,4,3:T(1,128)S(1)}, u32[]{:S(2)}, u32[]{:S(2)}) collective-permute-start(f32[6,1,3,5,2,256]{5,1,2,0,4,3:T(1,128)S(1)} %get-tuple-element.76), channel_id=1, source_target_pairs={{0,1},{1,2},{2,3},{4,5},{5,6},{6,7},{8,9},{9,10},{10,11},{12,13},{... | collective-permute-start | bytes 552968 | tf_op jit(solution)/shard_map/ppermute | solution.py:25
  56.7 6.9 %collective-permute-start.3 = (f32[6,1,3,5,2,256]{5,1,2,0,4,3:T(1,128)S(1)}, f32[6,1,3,5,2,256]{5,1,2,0,4,3:T(1,128)S(1)}, u32[]{:S(2)}, u32[]{:S(2)}) collective-permute-start(f32[6,1,3,5,2,256]{5,1,2,0,4,3:T(1,128)S(1)} %get-tuple-element.77), channel_id=1, source_target_pairs={{1,0},{2,1},{3,2},{5,4},{6,5},{7,6},{9,8},{10,9},{11,10},{13,12},{... | collective-permute-start | bytes 552968 | tf_op jit(solution)/shard_map/ppermute | solution.py:27
  59.2 73.3 %copy-start.9 = (f32[64,32]{0,1:T(8,128)S(1)}, f32[64,32]{0,1:T(8,128)}, u32[]{:S(2)}) copy-start(f32[64,32]{0,1:T(8,128)} %param.20) | copy-start | bytes 24580
  139.3 8.0 %slice-start.2 = ((s8[4423680]{0:T(1024)(128)(4,1)}), s8[4194304]{0:T(1024)(128)(4,1)S(1)}, s32[]{:S(2)}) async-start(s8[4423680]{0:T(1024)(128)(4,1)} %bitcast.163), calls=%async_computation.4 | async-start | bytes 8388608
  141.6 5.7 %slice-start.3 = ((s8[4423680]{0:T(1024)(128)(4,1)}), s8[229376]{0:T(1024)(128)(4,1)S(1)}, s32[]{:S(2)}) async-start(s8[4423680]{0:T(1024)(128)(4,1)} %bitcast.163), calls=%async_computation.5 | async-start | bytes 458752
  150.1 22.9 %collective-permute-start.4 = (f32[1,16,3,5,2,256]{5,1,2,4,3,0:T(8,128)S(1)}, f32[1,16,3,5,2,256]{5,1,2,4,3,0:T(8,128)S(1)}, u32[]{:S(2)}, u32[]{:S(2)}) collective-permute-start(f32[1,16,3,5,2,256]{5,1,2,4,3,0:T(8,128)S(1)} %get-tuple-element.80), channel_id=1, source_target_pairs={{0,4},{4,8},{8,12},{12,16},{16,20},{20,24},{24,28},{1,5},{5,9},{9,... | collective-permute-start | bytes 1474568 | tf_op jit(solution)/shard_map/ppermute | solution.py:25
  153.3 23.3 %collective-permute-start.5 = (f32[1,16,3,5,2,256]{5,1,2,0,4,3:T(8,128)S(1)}, f32[1,16,3,5,2,256]{5,1,2,0,4,3:T(8,128)S(1)}, u32[]{:S(2)}, u32[]{:S(2)}) collective-permute-start(f32[1,16,3,5,2,256]{5,1,2,0,4,3:T(8,128)S(1)} %get-tuple-element.81), channel_id=1, source_target_pairs={{4,0},{8,4},{12,8},{16,12},{20,16},{24,20},{28,24},{5,1},{9,5},{13... | collective-permute-start | bytes 1474568 | tf_op jit(solution)/shard_map/ppermute | solution.py:27
  176.8 5.9 %collective-permute-start.6 = (f32[6,1,3,5,2,256]{5,1,2,0,4,3:T(1,128)S(1)}, f32[6,1,3,5,2,256]{5,1,2,0,4,3:T(1,128)S(1)}, u32[]{:S(2)}, u32[]{:S(2)}) collective-permute-start(f32[6,1,3,5,2,256]{5,1,2,0,4,3:T(1,128)S(1)} %get-tuple-element.74), channel_id=1, source_target_pairs={{0,1},{1,2},{2,3},{4,5},{5,6},{6,7},{8,9},{9,10},{10,11},{12,13},{... | collective-permute-start | bytes 552968 | tf_op jit(solution)/shard_map/ppermute | solution.py:25
  180.3 6.9 %collective-permute-start.7 = (f32[6,1,3,5,2,256]{5,1,2,0,4,3:T(1,128)S(1)}, f32[6,1,3,5,2,256]{5,1,2,0,4,3:T(1,128)S(1)}, u32[]{:S(2)}, u32[]{:S(2)}) collective-permute-start(f32[6,1,3,5,2,256]{5,1,2,0,4,3:T(1,128)S(1)} %get-tuple-element.75), channel_id=1, source_target_pairs={{1,0},{2,1},{3,2},{5,4},{6,5},{7,6},{9,8},{10,9},{11,10},{13,12},{... | collective-permute-start | bytes 552968 | tf_op jit(solution)/shard_map/ppermute | solution.py:27
  194.9 9.0 %slice-start = ((s8[4423680]{0:T(1024)(128)(4,1)}), s8[4194304]{0:T(1024)(128)(4,1)S(1)}, s32[]{:S(2)}) async-start(s8[4423680]{0:T(1024)(128)(4,1)} %bitcast.161), calls=%async_computation.2 | async-start | bytes 8388608
  197.1 6.8 %slice-start.1 = ((s8[4423680]{0:T(1024)(128)(4,1)}), s8[229376]{0:T(1024)(128)(4,1)S(1)}, s32[]{:S(2)}) async-start(s8[4423680]{0:T(1024)(128)(4,1)} %bitcast.161), calls=%async_computation.3 | async-start | bytes 458752
  205.9 20.8 %collective-permute-start.8 = (f32[1,16,3,5,2,256]{5,1,4,3,2,0:T(8,128)S(1)}, f32[1,16,3,5,2,256]{5,1,4,3,2,0:T(8,128)S(1)}, u32[]{:S(2)}, u32[]{:S(2)}) collective-permute-start(f32[1,16,3,5,2,256]{5,1,4,3,2,0:T(8,128)S(1)} %get-tuple-element.78), channel_id=1, source_target_pairs={{0,4},{4,8},{8,12},{12,16},{16,20},{20,24},{24,28},{1,5},{5,9},{9,... | collective-permute-start | bytes 1474568 | tf_op jit(solution)/shard_map/ppermute | solution.py:25
  208.3 21.1 %collective-permute-start.9 = (f32[1,16,3,5,2,256]{5,1,4,3,2,0:T(8,128)S(1)}, f32[1,16,3,5,2,256]{5,1,4,3,2,0:T(8,128)S(1)}, u32[]{:S(2)}, u32[]{:S(2)}) collective-permute-start(f32[1,16,3,5,2,256]{5,1,4,3,2,0:T(8,128)S(1)} %get-tuple-element.79), channel_id=1, source_target_pairs={{4,0},{8,4},{12,8},{16,12},{20,16},{24,20},{28,24},{5,1},{9,5},{13... | collective-permute-start | bytes 1474568 | tf_op jit(solution)/shard_map/ppermute | solution.py:27
  229.6 4.4 %collective-permute-start.10 = (f32[6,1,3,5,2,256]{5,1,4,3,2,0:T(1,128)S(1)}, f32[6,1,3,5,2,256]{5,1,4,3,2,0:T(1,128)S(1)}, u32[]{:S(2)}, u32[]{:S(2)}) collective-permute-start(f32[6,1,3,5,2,256]{5,1,4,3,2,0:T(1,128)S(1)} %get-tuple-element.72), channel_id=1, source_target_pairs={{0,1},{1,2},{2,3},{4,5},{5,6},{6,7},{8,9},{9,10},{10,11},{12,13},{... | collective-permute-start | bytes 552968 | tf_op jit(solution)/shard_map/ppermute | solution.py:25
  231.5 6.9 %collective-permute-start.11 = (f32[6,1,3,5,2,256]{5,1,4,3,2,0:T(1,128)S(1)}, f32[6,1,3,5,2,256]{5,1,4,3,2,0:T(1,128)S(1)}, u32[]{:S(2)}, u32[]{:S(2)}) collective-permute-start(f32[6,1,3,5,2,256]{5,1,4,3,2,0:T(1,128)S(1)} %get-tuple-element.73), channel_id=1, source_target_pairs={{1,0},{2,1},{3,2},{5,4},{6,5},{7,6},{9,8},{10,9},{11,10},{13,12},{... | collective-permute-start | bytes 552968 | tf_op jit(solution)/shard_map/ppermute | solution.py:27
  246.2 3.2 %copy-start.2 = (f32[6,18,3,5,2,256]{5,1,4,3,2,0:T(8,128)S(1)}, f32[6,18,3,5,2,256]{5,1,4,3,2,0:T(8,128)}, u32[]{:S(2)}) copy-start(f32[6,18,3,5,2,256]{5,1,4,3,2,0:T(8,128)} %scatter.14) | copy-start | bytes 9953284
  253.3 2.1 copy-start.4
  259.1 4.3 %copy-start.1 = (f32[32,32]{1,0:T(8,128)S(1)}, f32[32,32]{1,0:T(8,128)}, u32[]{:S(2)}) copy-start(f32[32,32]{1,0:T(8,128)} %param.19) | copy-start | bytes 12292
  (6 other events, 7.5 us)
Sparse Core Ops, SparseCore 0:
  16.2 36.3 all-reduce.2
  56.1 76.3 all-reduce.4
